TPU v7x, 32 devices: a whole 2x2x4 slice. The times are simulated.
32 devices in a mesh: groups: 2 (over y), ctx: 4 (over z), head: 2 (over x), sub: 2 (over core).
Axes of the slice: x: 2, y: 2, z: 4, core: 2. Of those that a mesh axis runs over, the one named last changes fastest.
Arguments:
- queries: bfloat16 [3072, 8192], P(('groups', 'ctx'), ('head', 'sub')), parts along dimension 0, may hold values from -60 to 60
- key_rows: bfloat16 [3072, 1024], P(('groups', 'ctx'), 'head'), parts along dimension 0, may hold values from -6 to 6
- value_rows: bfloat16 [3072, 1024], P(('groups', 'ctx'), 'head'), parts along dimension 0, may hold values from -6 to 6
- out_weight: bfloat16 [8192, 5120], P(('head', 'sub'), 'ctx'), may hold values from -0.375 to 0.375
Outputs:
- mixed: bfloat16 [3072, 5120], P(('groups', 'ctx'), ('head', 'sub')), parts along dimension 0
There are 2 independent parts, one for each index of `groups`. A program takes and returns all parts, laid end to end along the dimension named above; an argument that names none is the same for every part. Nothing has to cross between parts.
All inputs are finite; a program needn't handle non-finite values.
Results may differ from a plain program's by a relative error of at most 0.02.
Values may be sent and summed in bfloat16 or wider, within the bound.
A program may use at most 128 MiB of HBM per device.

v0:
```python
import jax
import jax.numpy as jnp
from jax import lax
from jax.sharding import PartitionSpec as P

QH = 64
KVH = 8
HD = 128


def from_behind(block, axis, distance):
    devices = range(lax.axis_size(axis))
    route = [((i - distance) % len(devices), i) for i in devices]
    return lax.ppermute(block, axis, route)


def on_device(queries, key_rows, value_rows, out_weight):
    token_count = queries.shape[0]
    heads_here = queries.shape[1] // HD
    pairs_here = key_rows.shape[1] // HD
    group_ratio = QH // KVH
    pairs_read = max(heads_here // group_ratio, 1)
    per_pair = heads_here // pairs_read
    head_offset = lax.axis_index("sub") * heads_here // group_ratio
    keys_read = lax.dynamic_slice_in_dim(
        key_rows.reshape(token_count, pairs_here, HD), head_offset, pairs_read, 1
    )
    values_read = lax.dynamic_slice_in_dim(
        value_rows.reshape(token_count, pairs_here, HD), head_offset, pairs_read, 1
    )
    stacked = jnp.stack([keys_read, values_read])
    grouped = queries.reshape(token_count, pairs_read, per_pair, HD)
    factor = 1.0 / HD**0.5

    def absorb(running, key_block, value_block):
        old_max, old_sum, old_out = running
        scores = (
            jnp.einsum("tngd,knd->tngk", grouped, key_block, preferred_element_type=jnp.float32)
            * factor
        )
        new_max = jnp.maximum(old_max, jnp.max(scores, axis=-1))
        shrink = jnp.exp(old_max - new_max)
        expo = jnp.exp(scores - new_max[..., None])
        new_sum = old_sum * shrink + jnp.sum(expo, axis=-1)
        added = jnp.einsum(
            "tngk,knd->tngd",
            expo.astype(jnp.bfloat16),
            value_block,
            preferred_element_type=jnp.float32,
        )
        return (new_max, new_sum, old_out * shrink[..., None] + added)

    empty = (
        jnp.full((token_count, pairs_read, per_pair), -1e30, jnp.float32),
        jnp.zeros((token_count, pairs_read, per_pair), jnp.float32),
        jnp.zeros((token_count, pairs_read, per_pair, HD), jnp.float32),
    )
    cycle_size = lax.axis_size("ctx")

    def forward(blocks):
        return from_behind(blocks, "ctx", 1)

    def both_turn(turn_index, loop_state):
        ahead, behind, running = loop_state
        ahead = forward(ahead)
        behind = from_behind(behind, "ctx", -1)
        running = absorb(running, ahead[0], ahead[1])
        return (ahead, behind, absorb(running, behind[0], behind[1]))

    ahead, _, final = lax.fori_loop(
        0,
        (cycle_size - 1) // 2,
        both_turn,
        (stacked, stacked, absorb(empty, keys_read, values_read)),
    )
    ahead = forward(ahead)
    final = absorb(final, ahead[0], ahead[1])
    attended = (
        (final[2] / final[1][..., None]).astype(jnp.bfloat16).reshape(token_count, heads_here * HD)
    )
    partial_value = jnp.dot(
        attended,
        lax.all_gather(out_weight, "ctx", axis=1, tiled=True),
        preferred_element_type=jnp.float32,
    )
    summed = lax.psum_scatter(
        partial_value.astype(jnp.bfloat16), ("head", "sub"), scatter_dimension=1, tiled=True
    )
    return summed


def solution(mesh):
    return jax.shard_map(
        on_device,
        mesh=mesh,
        in_specs=(
            P(("groups", "ctx"), ("head", "sub")),
            P(("groups", "ctx"), "head"),
            P(("groups", "ctx"), "head"),
            P(("head", "sub"), "ctx"),
        ),
        out_specs=P(("groups", "ctx"), ("head", "sub")),
        check_vma=False,
    )
```

profile of v0, /device:TPU:3, one launch (start us, length us, event | category | flops | bytes accessed | tf_op | source)
XLA Modules:
  0.0 440.1 jit_solution(13286977916574830429)
XLA Ops:
  6.5 0.0 all-gather.2.cloned.1.call-start
  6.5 0.7 all-gather.2.cloned.1.call-update
  7.3 0.0 reduce-scatter.2.cloned.1.call-start
  7.3 1.2 copy.17
  8.5 1.2 copy.20
  9.8 0.2 copy.50
  10.0 0.2 copy.22
  10.2 1.3 collective-permute-start
  11.6 2.1 collective-permute-start.1
  13.6 0.0 copy-done
  13.6 0.4 copy.51
  14.1 1.5 bitcast_reduce_fusion.3
  15.6 6.6 %collective-permute-done = bf16[2,384,2,128]{3,1,2,0:T(8,128)(2,1)S(1)} collective-permute-done((bf16[2,384,2,128]{3,1,2,0:T(8,128)(2,1)S(1)}, bf16[2,384,2,128]{3,1,2,0:T(8,128)(2,1)S(1)}, u32[]{:S(2)}, u32[]{:S(2)}) %collective-permute-start) | collective-permute-done | bytes 393248 | tf_op jit(solution)/shard_map/while/body/eval_jaxpr/ppermute | solution.py:14
  22.2 0.0 collective-permute-start.2
  22.2 1.5 bitcast_reduce_fusion.2
  23.7 11.2 %collective-permute-done.1 = bf16[2,384,2,128]{3,1,2,0:T(8,128)(2,1)S(1)} collective-permute-done((bf16[2,384,2,128]{3,1,2,0:T(8,128)(2,1)S(1)}, bf16[2,384,2,128]{3,1,2,0:T(8,128)(2,1)S(1)}, u32[]{:S(2)}, u32[]{:S(2)}) %collective-permute-start.1) | collective-permute-done | bytes 393248 | tf_op jit(solution)/shard_map/while/body/eval_jaxpr/ppermute | solution.py:14
  34.9 5.1 %bitcast_reduce_fusion.1 = (f32[384,2,8]{0,2,1:T(8,128)S(1)}, f32[2,384,384,8]{2,1,3,0:T(8,128)}) fusion(bf16[384,2,8,128]{3,2,1,0:T(8,128)(2,1)S(1)} %bitcast.138, bf16[2,384,2,128]{3,1,2,0:T(8,128)(2,1)S(1)} %collective-permute-done.1), kind=kOutput, calls=%fused_computation.4 | convolution fusion | flops 608692224 | bytes 11231232 | tf_op jit(solution)/shard_map/while/body/eval_jaxpr/tngd,knd->tngk/dot_general | solution.py:38
  40.0 0.0 copy-done.1
  40.0 8.3 %collective-permute-done.2 = bf16[2,384,2,128]{3,1,2,0:T(8,128)(2,1)S(1)} collective-permute-done((bf16[2,384,2,128]{3,1,2,0:T(8,128)(2,1)S(1)}, bf16[2,384,2,128]{3,1,2,0:T(8,128)(2,1)S(1)}, u32[]{:S(2)}, u32[]{:S(2)}) %collective-permute-start.2) | collective-permute-done | bytes 393248 | tf_op jit(solution)/shard_map/ppermute | solution.py:14
  48.4 5.1 %bitcast_reduce_fusion = (f32[384,2,8]{0,2,1:T(8,128)S(1)}, f32[2,384,384,8]{2,1,3,0:T(8,128)}) fusion(bf16[384,2,8,128]{3,2,1,0:T(8,128)(2,1)S(1)} %bitcast.139, bf16[2,384,2,128]{3,1,2,0:T(8,128)(2,1)S(1)} %collective-permute-done.2), kind=kOutput, calls=%fused_computation.1 | convolution fusion | flops 608692224 | bytes 11231232 | tf_op jit(solution)/shard_map/tngd,knd->tngk/dot_general | solution.py:38
  53.4 0.0 copy-done.3
  53.4 1.6 fusion.4
  55.0 0.0 copy-done.5
  55.0 1.6 fusion.6
  56.6 5.3 %fusion.8 = f32[384,2,8]{0,2,1:T(8,128)S(1)} fusion(f32[2,384,384,8]{2,1,3,0:T(8,128)} %get-tuple-element.38, f32[384,2,8]{0,2,1:T(8,128)S(1)} %get-tuple-element.30), kind=kLoop, calls=%fused_computation.16 | loop fusion | flops 7071744 | bytes 9486336 | tf_op jit(solution)/shard_map/while/body/eval_jaxpr/reduce_sum | solution.py:44
  62.0 5.3 %fusion.10 = f32[384,2,8]{0,2,1:T(8,128)S(1)} fusion(f32[2,384,384,8]{2,1,3,0:T(8,128)} %get-tuple-element.36, f32[384,2,8]{0,2,1:T(8,128)S(1)} %get-tuple-element.28), kind=kLoop, calls=%fused_computation.18 | loop fusion | flops 7071744 | bytes 9486336 | tf_op jit(solution)/shard_map/reduce_sum | solution.py:44
  67.2 0.0 copy-start.2
  67.2 0.7 multiply_add_fusion
  67.9 2.1 fusion.18
  69.9 0.0 copy-done.2
  70.0 0.0 slice-start.2
  70.0 0.0 copy-start.4
  70.0 0.0 slice-start.3
  70.0 0.0 slice-start.4
  70.0 1.8 fusion.16
  71.8 0.0 slice-done
  71.8 0.0 slice-done.1
  71.8 0.0 slice-done.2
  71.8 0.1 copy-done.4
  71.9 1.7 fusion.14
  73.7 1.1 slice-done.5
  74.8 0.0 copy-done.9
  74.8 0.0 copy-done.10
  74.8 3.6 fusion.29
  78.4 299.4 %all-gather.2.cloned.1.call-done = bf16[2048,5120]{1,0:T(8,128)(2,1)} async-done(((bf16[2048,1280]{1,0:T(8,128)(2,1)}), bf16[2048,5120]{1,0:T(8,128)(2,1)}) %all-gather.2.cloned.1.call-update) | async-done | bytes 20971536 | tf_op jit(solution)/shard_map/all_gather | solution.py:83
  377.8 14.5 %convolution_convert_fusion = bf16[384,5120]{1,0:T(8,128)(2,1)} fusion(bf16[384,2048]{0,1:T(8,128)(2,1)} %bitcast.147, bf16[2048,5120]{1,0:T(8,128)(2,1)} %all-gather.2.cloned.1.call-done), kind=kOutput, calls=%fused_computation.20 | convolution fusion | flops 8055029760 | bytes 26476544 | tf_op jit(solution)/shard_map/dot_general | solution.py:81
  392.3 0.0 reduce-scatter.2.cloned.1.call-update
  392.3 41.0 %reduce-scatter.2.cloned.1.call-done = bf16[384,1280]{1,0:T(8,128)(2,1)} async-done(((bf16[384,5120]{1,0:T(8,128)(2,1)}), bf16[384,1280]{1,0:T(8,128)(2,1)}) %reduce-scatter.2.cloned.1.call-update) | async-done | bytes 983056 | tf_op jit(solution)/shard_map/reduce_scatter | solution.py:86
  (22 shorter events, 0.1 us)
Async XLA Ops:
  6.5 7.1 %copy-start = (bf16[384,2048]{1,0:T(8,128)(2,1)S(1)}, bf16[384,2048]{1,0:T(8,128)(2,1)}, u32[]{:S(2)}) copy-start(bf16[384,2048]{1,0:T(8,128)(2,1)} %param.4) | copy-start | bytes 4718596
  6.5 371.3 %all-gather.2.cloned.1.call-start = ((), (), s32[]{:S(2)}) async-start(), calls=%async_computation.1 | async-start | bytes 26214400 | tf_op jit(solution)/shard_map/all_gather | solution.py:83
  7.3 426.0 %reduce-scatter.2.cloned.1.call-start = ((), (), s32[]{:S(2)}) async-start(), calls=%async_computation.2 | async-start | bytes 4915200 | tf_op jit(solution)/shard_map/reduce_scatter | solution.py:86
  10.2 12.0 %collective-permute-start = (bf16[2,384,2,128]{3,1,2,0:T(8,128)(2,1)S(1)}, bf16[2,384,2,128]{3,1,2,0:T(8,128)(2,1)S(1)}, u32[]{:S(2)}, u32[]{:S(2)}) collective-permute-start(bf16[2,384,2,128]{3,1,2,0:T(8,128)(2,1)S(1)} %pad_maximum_fusion), channel_id=1, source_target_pairs={{12,0},{0,4},{4,8},{8,12},{13,1},{1,5},{5,9},{9,13},{14,2},{2,6},{... | collective-permute-start | bytes 1179656 | tf_op jit(solution)/shard_map/while/body/eval_jaxpr/ppermute | solution.py:14
  11.6 23.4 %collective-permute-start.1 = (bf16[2,384,2,128]{3,1,2,0:T(8,128)(2,1)S(1)}, bf16[2,384,2,128]{3,1,2,0:T(8,128)(2,1)S(1)}, u32[]{:S(2)}, u32[]{:S(2)}) collective-permute-start(bf16[2,384,2,128]{3,1,2,0:T(8,128)(2,1)S(1)} %pad_maximum_fusion), channel_id=1, source_target_pairs={{4,0},{8,4},{12,8},{0,12},{5,1},{9,5},{13,9},{1,13},{6,2},{10,6},{... | collective-permute-start | bytes 1179656 | tf_op jit(solution)/shard_map/while/body/eval_jaxpr/ppermute | solution.py:14
  22.2 17.8 %copy-start.1 = (bf16[2,384,2,128]{3,1,2,0:T(8,128)(2,1)}, bf16[2,384,2,128]{3,1,2,0:T(8,128)(2,1)S(1)}, u32[]{:S(2)}) copy-start(bf16[2,384,2,128]{3,1,2,0:T(8,128)(2,1)S(1)} %collective-permute-done) | copy-start | bytes 1179652
  22.2 26.1 %collective-permute-start.2 = (bf16[2,384,2,128]{3,1,2,0:T(8,128)(2,1)S(1)}, bf16[2,384,2,128]{3,1,2,0:T(8,128)(2,1)S(1)}, u32[]{:S(2)}, u32[]{:S(2)}) collective-permute-start(bf16[2,384,2,128]{3,1,2,0:T(8,128)(2,1)S(1)} %collective-permute-done), channel_id=1, source_target_pairs={{12,0},{0,4},{4,8},{8,12},{13,1},{1,5},{5,9},{9,13},{14,2},{2,6},{... | collective-permute-start | bytes 1179656 | tf_op jit(solution)/shard_map/ppermute | solution.py:14
  34.9 18.5 %copy-start.3 = (bf16[2,384,2,128]{3,1,2,0:T(8,128)(2,1)}, bf16[2,384,2,128]{3,1,2,0:T(8,128)(2,1)S(1)}, u32[]{:S(2)}) copy-start(bf16[2,384,2,128]{3,1,2,0:T(8,128)(2,1)S(1)} %collective-permute-done.1) | copy-start | bytes 1179652
  48.4 6.7 %copy-start.5 = (bf16[2,384,2,128]{3,1,2,0:T(8,128)(2,1)}, bf16[2,384,2,128]{3,1,2,0:T(8,128)(2,1)S(1)}, u32[]{:S(2)}) copy-start(bf16[2,384,2,128]{3,1,2,0:T(8,128)(2,1)S(1)} %collective-permute-done.2) | copy-start | bytes 1179652
  67.2 2.7 copy-start.2
  67.9 3.9 slice-start
  67.9 3.9 slice-start.1
  70.0 1.9 slice-start.2
  70.0 1.9 copy-start.4
  70.0 3.7 slice-start.3
  70.0 3.7 slice-start.4
  71.9 2.9 slice-start.5
  71.9 2.9 copy-start.6
  71.9 2.9 copy-start.7
  71.9 2.9 copy-start.8
  71.9 2.9 copy-start.9
  71.9 2.9 copy-start.10
Sparse Core Ops, SparseCore 0:
  8.9 368.8 all-gather.1
  392.5 40.7 reduce-scatter.1
where the time goes:
time: 443 us; the launch traced here: 440 us
  waiting for transfers between devices  367 us (83%)
  matrix products  36.8 us (8%)
  other arithmetic  14.5 us (3%)
  between operations  13.7 us (3%)
  local copies, waits for them, and re-layouts  4.46 us (1%)
    all_gather x1, waiting for transfers between devices, on_device(): lax.all_gather(out_weight, 'ctx', axis=1, tiled=True)  299 us
    reduce_scatter x1, waiting for transfers between devices, on_device(): lax.psum_scatter(partial_value.astype(jnp.bfloat16), ('head', 'sub'), sca...  41 us
    ppermute x3, waiting for transfers between devices, from_behind(): return lax.ppermute(block, axis, route)  26.1 us
    dot_general x1, matrix products, on_device(): jnp.dot(attended, lax.all_gather(out_weight, 'ctx', axis=1, tiled=True),...  14.5 us
    reduce_sum x4, other arithmetic, absorb(): new_sum = old_sum * shrink + jnp.sum(expo, axis=-1)  13.8 us
    dot_general x4, matrix products, absorb(): jnp.einsum('tngd,knd->tngk', grouped, key_block, preferred_element_type=j...  13.2 us
    dot_general x4, matrix products, absorb(): jnp.einsum('tngk,knd->tngd', expo.astype(jnp.bfloat16), value_block, pref...  9.14 us
  transfers between devices with their start and end apart: 5, of which 5 were waited for; matrix products, arithmetic and copies ran while one was open for 9% of the time, Pallas kernels for 0%

commit v1 on v0

v1 whole, which is shorter than its diff:
```python
import functools
import math

import jax
import jax.numpy as jnp
from jax import lax
from jax.experimental import pallas as pl
from jax.experimental.pallas import tpu as pltpu
from jax.sharding import PartitionSpec as P

QH = 64
KVH = 8
HD = 128
CHUNKS = 2
ROWS = 128


def attend_kernel(q_ref, k_ref, v_ref, o_ref, v_ext):
    v_ext[:, :HD] = v_ref[...]
    v_ext[:, HD:] = jnp.ones((v_ref.shape[0], HD), v_ref.dtype)
    factor = math.log2(math.e) / HD**0.5
    for start in range(0, q_ref.shape[0], ROWS):
        rows = pl.ds(start, ROWS)
        scores = lax.dot_general(
            q_ref[rows, :], k_ref[...], (((1,), (1,)), ((), ())), preferred_element_type=jnp.float32
        )
        row_max = jnp.max(scores, axis=1, keepdims=True)
        weights = jnp.exp2((scores - row_max) * factor).astype(jnp.bfloat16)
        both = jnp.dot(weights, v_ext[...], preferred_element_type=jnp.float32)
        o_ref[rows, :] = (both[:, :HD] / both[:, HD:]).astype(o_ref.dtype)


def attend(queries, key_value, first_head, heads, per_pair, pairs):
    tokens = queries.shape[0]
    keys = key_value.shape[0]
    return pl.pallas_call(
        attend_kernel,
        grid=(heads,),
        out_shape=jax.ShapeDtypeStruct((tokens, heads * HD), jnp.bfloat16),
        in_specs=[
            pl.BlockSpec((tokens, HD), lambda h: (0, first_head + h)),
            pl.BlockSpec((keys, HD), lambda h: (0, (first_head + h) // per_pair)),
            pl.BlockSpec((keys, HD), lambda h: (0, pairs + (first_head + h) // per_pair)),
        ],
        out_specs=pl.BlockSpec((tokens, HD), lambda h: (0, h)),
        scratch_shapes=[pltpu.VMEM((keys, 2 * HD), jnp.bfloat16)],
        compiler_params=pltpu.CompilerParams(vmem_limit_bytes=48 * 2**20),
        cost_estimate=pl.CostEstimate(
            flops=8 * heads * tokens * keys * HD,
            bytes_accessed=4 * tokens * heads * HD + 4 * keys * HD,
            transcendentals=heads * tokens * keys,
        ),
    )(queries, key_value, key_value)


def on_device(queries, key_rows, value_rows, out_weight):
    token_count = queries.shape[0]
    heads_here = queries.shape[1] // HD
    group_ratio = QH // KVH
    pairs_read = max(heads_here // group_ratio, 1)
    per_pair = heads_here // pairs_read
    head_offset = lax.axis_index("sub") * heads_here // group_ratio
    key_value = jnp.concatenate(
        [
            lax.dynamic_slice_in_dim(rows, head_offset * HD, pairs_read * HD, 1)
            for rows in (key_rows, value_rows)
        ],
        axis=1,
    )
    key_value = lax.all_gather(key_value, "ctx", axis=0, tiled=True)
    heads = heads_here // CHUNKS
    partial_value = None
    for chunk in range(CHUNKS):
        attended = attend(queries, key_value, chunk * heads, heads, per_pair, pairs_read)
        everyone = lax.all_gather(attended, "ctx", axis=0, tiled=True)
        rows = out_weight[chunk * heads * HD : (chunk + 1) * heads * HD]
        added = jnp.dot(everyone, rows, preferred_element_type=jnp.float32)
        partial_value = added if partial_value is None else partial_value + added
    summed = lax.psum_scatter(
        partial_value.astype(jnp.bfloat16), ("head", "sub"), scatter_dimension=0, tiled=True
    )
    size = lax.axis_size("ctx")
    route = [(a * size + b, b * size + a) for a in range(size) for b in range(size)]
    return lax.ppermute(summed, ("ctx", "head", "sub"), route)


def solution(mesh):
    assert mesh.shape["ctx"] == mesh.shape["head"] * mesh.shape["sub"]
    return jax.shard_map(
        on_device,
        mesh=mesh,
        in_specs=(
            P(("groups", "ctx"), ("head", "sub")),
            P(("groups", "ctx"), "head"),
            P(("groups", "ctx"), "head"),
            P(("head", "sub"), "ctx"),
        ),
        out_specs=P(("groups", "ctx"), ("head", "sub")),
        check_vma=False,
    )
```

time: 443 us -> 296 us (0.67)
  the two profiles are of different devices: /device:TPU:3 before, /device:TPU:2 now
where the time goes in v1:
time: 296 us
  waiting for transfers between devices  228 us (77%)
  Pallas kernels  22.7 us (8%)
  matrix products  21.3 us (7%)
  between operations  13.2 us (4%)
  starting transfers between devices  5.55 us (2%)
  local copies, waits for them, and re-layouts  4.81 us (2%)
    all_gather x2, waiting for transfers between devices, on_device(): everyone = lax.all_gather(attended, 'ctx', axis=0, tiled=True)  104 us
    ppermute x1, waiting for transfers between devices, on_device(): return lax.ppermute(summed, ('ctx', 'head', 'sub'), route)  43.8 us
    reduce_scatter x1, waiting for transfers between devices, on_device(): lax.psum_scatter(partial_value.astype(jnp.bfloat16), ('head', 'sub'), sca...  40.6 us
    all_gather x1, waiting for transfers between devices, on_device(): key_value = lax.all_gather(key_value, 'ctx', axis=0, tiled=True)  38.7 us
    pallas_call x2, Pallas kernels, attend(): pl.pallas_call(attend_kernel, grid=(heads,), out_shape=jax.ShapeDtypeStru...  22.7 us
    dot_general x2, matrix products, on_device(): added = jnp.dot(everyone, rows, preferred_element_type=jnp.float32)  21.3 us
  transfers between devices with their start and end apart: 5, of which 5 were waited for; matrix products, arithmetic and copies ran while one was open for 3% of the time, Pallas kernels for 4%

profile of v1, /device:TPU:2, one launch (start us, length us, event | category | flops | bytes accessed | tf_op | source)
XLA Modules:
  0.0 296.0 jit_solution(15939995940420289074)
XLA Ops:
  6.5 0.0 all-gather.4.cloned.1.call-start
  6.5 1.0 constant_dynamic-slice_fusion
  7.6 0.8 pad_maximum_fusion
  8.4 0.0 all-gather.4.cloned.1.call-update
  8.4 0.0 all-gather.6.cloned.1.call-start
  8.4 38.7 %all-gather.4.cloned.1.call-done.k_ref.v_ref = bf16[1536,512]{1,0:T(8,128)(2,1)} async-done(((bf16[384,512]{1,0:T(8,128)(2,1)}), bf16[1536,512]{1,0:T(8,128)(2,1)}) %all-gather.4.cloned.1.call-update) | async-done | bytes 1572880 | tf_op jit(solution)/shard_map/all_gather | solution.py:70
  47.2 0.0 copy-start
  47.2 1.4 copy-done
  48.6 0.0 copy-start.2
  48.6 1.4 copy-done.2
  50.0 0.0 copy-start.1
  50.0 0.0 copy-start.3
  50.0 11.3 %shard_map.46 = bf16[384,1024]{1,0:T(8,128)(2,1)} custom-call(bf16[384,2048]{1,0:T(8,128)(2,1)S(1)} %copy-done, bf16[1536,512]{1,0:T(8,128)(2,1)S(1)} %copy-done.2, bf16[1536,512]{1,0:T(8,128)(2,1)S(1)} %copy-done.2), custom_call_target="tpu_custom_call" | custom-call | flops 4831838208 | bytes 2359296 | tf_op jit(solution)/shard_map/pallas_call | solution.py:36
  61.3 0.0 all-gather.6.cloned.1.call-update
  61.3 0.0 all-gather.8.cloned.1.call-start
  61.4 0.0 copy-done.1
  61.4 0.0 copy-done.3
  61.4 11.4 %shard_map.47 = bf16[384,1024]{1,0:T(8,128)(2,1)} custom-call(bf16[384,2048]{1,0:T(8,128)(2,1)S(1)} %copy-done.1, bf16[1536,512]{1,0:T(8,128)(2,1)S(1)} %copy-done.3, bf16[1536,512]{1,0:T(8,128)(2,1)S(1)} %copy-done.3), custom_call_target="tpu_custom_call" | custom-call | flops 4831838208 | bytes 2359296 | tf_op jit(solution)/shard_map/pallas_call | solution.py:36
  72.8 0.0 all-gather.8.cloned.1.call-update
  72.8 0.0 reduce-scatter.2.cloned.1.call-start
  72.8 50.9 %all-gather.6.cloned.1.call-done = bf16[1536,1024]{1,0:T(8,128)(2,1)} async-done(((bf16[384,1024]{1,0:T(8,128)(2,1)}), bf16[1536,1024]{1,0:T(8,128)(2,1)}) %all-gather.6.cloned.1.call-update) | async-done | bytes 3145744 | tf_op jit(solution)/shard_map/all_gather | solution.py:75
  123.8 10.2 %fusion.2 = f32[1536,1280]{1,0:T(8,128)} fusion(bf16[1536,1024]{1,0:T(8,128)(2,1)} %all-gather.6.cloned.1.call-done, bf16[2048,1280]{1,0:T(8,128)(2,1)} %param.7), kind=kOutput, calls=%fused_computation.3 | convolution fusion | flops 4026531840 | bytes 13631488 | tf_op jit(solution)/shard_map/dot_general | solution.py:77
  133.9 53.5 %all-gather.8.cloned.1.call-done = bf16[1536,1024]{1,0:T(8,128)(2,1)} async-done(((bf16[384,1024]{1,0:T(8,128)(2,1)}), bf16[1536,1024]{1,0:T(8,128)(2,1)}) %all-gather.8.cloned.1.call-update) | async-done | bytes 3145744 | tf_op jit(solution)/shard_map/all_gather | solution.py:75
  187.5 11.2 %fusion = bf16[1536,1280]{1,0:T(8,128)(2,1)} fusion(f32[1536,1280]{1,0:T(8,128)} %fusion.2, bf16[1536,1024]{1,0:T(8,128)(2,1)} %all-gather.8.cloned.1.call-done, bf16[2048,1280]{1,0:T(8,128)(2,1)} %param.7), kind=kOutput, calls=%fused_computation.1 | convolution fusion | flops 4030464000 | bytes 17563648 | tf_op jit(solution)/shard_map/dot_general | solution.py:77
  198.6 0.0 reduce-scatter.2.cloned.1.call-update
  198.7 40.6 %reduce-scatter.2.cloned.1.call-done = bf16[384,1280]{1,0:T(8,128)(2,1)} async-done(((bf16[1536,1280]{1,0:T(8,128)(2,1)}), bf16[384,1280]{1,0:T(8,128)(2,1)}) %reduce-scatter.2.cloned.1.call-update) | async-done | bytes 983056 | tf_op jit(solution)/shard_map/reduce_scatter | solution.py:79
  239.3 5.4 %collective-permute-start = (bf16[384,1280]{1,0:T(8,128)(2,1)}, bf16[384,1280]{1,0:T(8,128)(2,1)S(1)}, u32[]{:S(2)}, u32[]{:S(2)}) collective-permute-start(bf16[384,1280]{1,0:T(8,128)(2,1)} %reduce-scatter.2.cloned.1.call-done), channel_id=1, source_target_pairs={{0,0},{1,4},{2,8},{3,12},{4,1},{5,5},{6,9},{7,13},{8,2},{9,6},{10,... | collective-permute-start | bytes 2949128 | tf_op jit(solution)/shard_map/ppermute | solution.py:84
  244.7 43.8 %collective-permute-done = bf16[384,1280]{1,0:T(8,128)(2,1)S(1)} collective-permute-done((bf16[384,1280]{1,0:T(8,128)(2,1)}, bf16[384,1280]{1,0:T(8,128)(2,1)S(1)}, u32[]{:S(2)}, u32[]{:S(2)}) %collective-permute-start) | collective-permute-done | bytes 983072 | tf_op jit(solution)/shard_map/ppermute | solution.py:84
  288.5 0.9 copy.6
Async XLA Ops:
  6.5 40.6 %all-gather.4.cloned.1.call-start = ((), (), s32[]{:S(2)}) async-start(), calls=%async_computation.1 | async-start | bytes 1966080 | tf_op jit(solution)/shard_map/all_gather | solution.py:70
  8.4 115.4 %all-gather.6.cloned.1.call-start = ((), (), s32[]{:S(2)}) async-start(), calls=%async_computation.2 | async-start | bytes 3932160 | tf_op jit(solution)/shard_map/all_gather | solution.py:75
  47.2 1.4 copy-start
  48.6 1.4 copy-start.2
  50.0 11.4 %copy-start.1 = (bf16[384,2048]{1,0:T(8,128)(2,1)S(1)}, bf16[384,2048]{1,0:T(8,128)(2,1)}, u32[]{:S(2)}) copy-start(bf16[384,2048]{1,0:T(8,128)(2,1)} %q_ref.3) | copy-start | bytes 4718596
  50.0 11.4 %copy-start.3 = (bf16[1536,512]{1,0:T(8,128)(2,1)S(1)}, bf16[1536,512]{1,0:T(8,128)(2,1)}, u32[]{:S(2)}) copy-start(bf16[1536,512]{1,0:T(8,128)(2,1)} %all-gather.4.cloned.1.call-done.k_ref.v_ref) | copy-start | bytes 4718596
  61.3 126.2 %all-gather.8.cloned.1.call-start = ((), (), s32[]{:S(2)}) async-start(), calls=%async_computation.3 | async-start | bytes 3932160 | tf_op jit(solution)/shard_map/all_gather | solution.py:75
  72.8 166.5 %reduce-scatter.2.cloned.1.call-start = ((), (), s32[]{:S(2)}) async-start(), calls=%async_computation.4 | async-start | bytes 4915200 | tf_op jit(solution)/shard_map/reduce_scatter | solution.py:79
  239.3 49.2 %collective-permute-start = (bf16[384,1280]{1,0:T(8,128)(2,1)}, bf16[384,1280]{1,0:T(8,128)(2,1)S(1)}, u32[]{:S(2)}, u32[]{:S(2)}) collective-permute-start(bf16[384,1280]{1,0:T(8,128)(2,1)} %reduce-scatter.2.cloned.1.call-done), channel_id=1, source_target_pairs={{0,0},{1,4},{2,8},{3,12},{4,1},{5,5},{6,9},{7,13},{8,2},{9,6},{10,... | collective-permute-start | bytes 2949128 | tf_op jit(solution)/shard_map/ppermute | solution.py:84
Sparse Core Ops, SparseCore 0:
  8.9 38.2 all-gather.3
  61.4 62.2 all-gather.5
  125.4 62.0 all-gather.7
  198.8 40.4 reduce-scatter.1

commit v2 on v1

v2 whole, which is shorter than its diff:
```python
import functools
import math

import jax
import jax.numpy as jnp
from jax import lax
from jax.experimental import pallas as pl
from jax.experimental.pallas import tpu as pltpu
from jax.sharding import PartitionSpec as P

QH = 64
KVH = 8
HD = 128
CHUNKS = 4
ROWS = 128
MESH = pl.DeviceIdType.MESH


def kernel(
    n, n_head, per_pair, pairs, kv_ref, q_ref, w_hbm, o_ref,
    kv_all, v_ext, att, w, own, out, rx1, summed, rx2, final,
    w_sem, kv_send, kv_recv, a_send, a_recv, s1, r1, s2, r2, s3, r3,
):
    me, head, sub = (lax.axis_index(a) for a in ("ctx", "head", "sub"))
    other = 1 - sub
    hs = head * 2 + sub
    tokens, width = q_ref.shape
    heads = width // HD
    columns = w.shape[1]
    piece = width // CHUNKS
    to_right, to_left = me < n - 1, me > 0
    right, left = lax.min(me + 1, n - 1), lax.max(me - 1, 0)
    away = hs != me
    turned = {"ctx": hs, "head": me // 2, "sub": me % 2}

    load_w = pltpu.make_async_copy(w_hbm, w, w_sem)
    load_w.start()

    barrier = pltpu.get_barrier_semaphore()

    def greet(where):
        pl.semaphore_signal(barrier, inc=1, device_id=where, device_id_type=MESH)

    pl.when(to_right)(lambda: greet({"ctx": right}))
    pl.when(to_left)(lambda: greet({"ctx": left}))
    pl.when(away)(lambda: greet(turned))
    greet({"sub": other})
    for step in range(1, n_head):
        greet({"head": lax.rem(head + step, n_head)})
    count = n_head + to_right.astype(jnp.int32) + to_left.astype(jnp.int32)
    pl.semaphore_wait(barrier, count + away.astype(jnp.int32))

    def remote(src, dst, send, recv, where):
        return pltpu.make_async_remote_copy(
            src_ref=src, dst_ref=dst, send_sem=send, recv_sem=recv, device_id=where, device_id_type=MESH
        )

    def rows_of(b):
        return pl.ds(pl.multiple_of(b * tokens, tokens), tokens)

    def kv_copy(src, b, way, d):
        where = {"ctx": right if way == 0 else left}
        return remote(src, kv_all.at[rows_of(b)], kv_send.at[way, d], kv_recv.at[b], where)

    pl.when(to_right)(lambda: kv_copy(kv_ref, me, 0, 0).start())
    pl.when(to_left)(lambda: kv_copy(kv_ref, me, 1, 0).start())
    kv_all[rows_of(me), :] = kv_ref[...]

    @pl.loop(1, n)
    def _(d):
        @pl.when(me - d >= 0)
        def _():
            copy = kv_copy(kv_all.at[rows_of(me - d)], me - d, 0, d)
            copy.wait_recv()
            pl.when(to_right)(lambda: copy.start())

        @pl.when(me + d < n)
        def _():
            copy = kv_copy(kv_all.at[rows_of(me + d)], me + d, 1, d)
            copy.wait_recv()
            pl.when(to_left)(lambda: copy.start())

    for p in range(pairs):
        v_ext[p, :, :HD] = kv_all[:, (pairs + p) * HD : (pairs + p + 1) * HD]
        v_ext[p, :, HD:] = jnp.ones((v_ext.shape[1], HD), v_ext.dtype)

    def a_copy(b, j, way, d):
        where = {"ctx": right if way == 0 else left}
        part = att.at[b, :, pl.ds(j * piece, piece)]
        return remote(part, part, a_send.at[way, d, j], a_recv.at[b, j], where)

    factor = math.log2(math.e) / HD**0.5
    for j in range(CHUNKS):

        @pl.loop(j * heads // CHUNKS, (j + 1) * heads // CHUNKS)
        def _(h):
            pair = h // per_pair
            cols = pl.ds(pl.multiple_of(h * HD, HD), HD)
            keys = kv_all[:, pl.ds(pl.multiple_of(pair * HD, HD), HD)]
            for start in range(0, tokens, ROWS):
                rows = pl.ds(start, ROWS)
                scores = lax.dot_general(
                    q_ref[rows, cols], keys, (((1,), (1,)), ((), ())), preferred_element_type=jnp.float32
                )
                row_max = jnp.max(scores, axis=1, keepdims=True)
                weights = jnp.exp2((scores - row_max) * factor).astype(jnp.bfloat16)
                both = jnp.dot(weights, v_ext[pair], preferred_element_type=jnp.float32)
                att[me, rows, cols] = (both[:, :HD] / both[:, HD:]).astype(att.dtype)

        pl.when(to_right)(lambda: a_copy(me, j, 0, 0).start())
        pl.when(to_left)(lambda: a_copy(me, j, 1, 0).start())

    load_w.wait()
    tile = 256 if columns % 256 == 0 else columns

    def product(t, dst):
        if tile == columns:
            dst[...] = jnp.dot(att[t], w[...], preferred_element_type=jnp.float32).astype(dst.dtype)
        else:

            @pl.loop(0, columns // tile)
            def _(c):
                cols = pl.ds(pl.multiple_of(c * tile, tile), tile)
                dst[:, cols] = jnp.dot(
                    att[t], w[:, cols], preferred_element_type=jnp.float32
                ).astype(dst.dtype)

    def core_copy(g):
        return remote(out.at[g], rx1.at[g], s1.at[g], r1.at[g], {"sub": other})

    def head_copy(g):
        return remote(summed.at[g], rx2.at[head], s2.at[g], r2.at[head], {"head": g})

    def last_copy():
        return remote(final, o_ref, s3, r3, turned)

    def multiply(t):
        g = t // 2

        @pl.when(t % 2 == sub)
        def _():
            product(t, own.at[g])

        @pl.when(t % 2 != sub)
        def _():
            product(t, out.at[g])
            core_copy(g).start()

    def combine(t):
        g = t // 2

        @pl.when(t % 2 == sub)
        def _():
            core_copy(g).wait_recv()
            summed[g] = (own[g].astype(jnp.float32) + rx1[g].astype(jnp.float32)).astype(summed.dtype)
            pl.when(g != head)(lambda: head_copy(g).start())

    def finish():
        for step in range(1, n_head):
            source = lax.rem(head + step, n_head)
            remote(
                summed.at[source], rx2.at[source], s2.at[source], r2.at[source], {"head": source}
            ).wait_recv()
        for start in range(0, tokens, ROWS):
            rows = pl.ds(start, ROWS)
            total = summed[head, rows, :].astype(jnp.float32)
            for step in range(1, n_head):
                total += rx2[lax.rem(head + step, n_head), rows, :].astype(jnp.float32)
            final[rows, :] = total.astype(final.dtype)
        pl.when(away)(lambda: last_copy().start())

    multiply(me)
    combine(me)
    gap = lax.max(hs - me, me - hs)

    @pl.loop(1, n)
    def _(d):
        for j in range(CHUNKS):

            @pl.when(me - d >= 0)
            def _():
                copy = a_copy(me - d, j, 0, d)
                copy.wait_recv()
                pl.when(to_right)(lambda: copy.start())

            @pl.when(me + d < n)
            def _():
                copy = a_copy(me + d, j, 1, d)
                copy.wait_recv()
                pl.when(to_left)(lambda: copy.start())

        pl.when(me - d >= 0)(lambda: multiply(me - d))
        pl.when(me + d < n)(lambda: multiply(me + d))
        pl.when(me - d >= 0)(lambda: combine(me - d))
        pl.when(me + d < n)(lambda: combine(me + d))
        pl.when(gap == d - 1)(finish)

    pl.when(gap == n - 1)(finish)

    @pl.when(away)
    def _():
        last_copy().wait()

    @pl.when(jnp.logical_not(away))
    def _():
        o_ref[...] = final[...]

    @pl.loop(0, n)
    def _(d):
        for way, fits, go in ((0, me - d >= 0, to_right), (1, me + d < n, to_left)):
            b = me - d if way == 0 else me + d

            @pl.when(jnp.logical_and(fits, go))
            def _():
                kv_copy(kv_all.at[rows_of(b)], b, way, d).wait_send()
                for j in range(CHUNKS):
                    a_copy(b, j, way, d).wait_send()

    @pl.loop(0, n // 2)
    def _(g):
        core_copy(g).wait_send()
        pl.when(g != head)(lambda: head_copy(g).wait_send())


def on_device(queries, key_rows, value_rows, out_weight):
    tokens, width = queries.shape
    heads_here = width // HD
    group_ratio = QH // KVH
    pairs = max(heads_here // group_ratio, 1)
    per_pair = heads_here // pairs
    head_offset = lax.axis_index("sub") * heads_here // group_ratio
    key_value = jnp.concatenate(
        [
            lax.dynamic_slice_in_dim(rows, head_offset * HD, pairs * HD, 1)
            for rows in (key_rows, value_rows)
        ],
        axis=1,
    )
    n = lax.axis_size("ctx")
    n_head = lax.axis_size("head")
    columns = out_weight.shape[1]
    block = (tokens, columns)
    groups = (n // 2,) + block
    vmem = pl.BlockSpec(memory_space=pltpu.VMEM)
    dma = pltpu.SemaphoreType.DMA
    bf16 = jnp.bfloat16
    return pl.pallas_call(
        functools.partial(kernel, n, n_head, per_pair, pairs),
        out_shape=jax.ShapeDtypeStruct(block, bf16),
        in_specs=[vmem, vmem, pl.BlockSpec(memory_space=pl.ANY)],
        out_specs=vmem,
        scratch_shapes=[
            pltpu.VMEM((n * tokens, 2 * pairs * HD), bf16),
            pltpu.VMEM((pairs, n * tokens, 2 * HD), bf16),
            pltpu.VMEM((n, tokens, width), bf16),
            pltpu.VMEM(out_weight.shape, bf16),
            pltpu.VMEM(groups, bf16),
            pltpu.VMEM(groups, bf16),
            pltpu.VMEM(groups, bf16),
            pltpu.VMEM(groups, bf16),
            pltpu.VMEM((n_head,) + block, bf16),
            pltpu.VMEM(block, bf16),
            dma,
            dma((2, n)),
            dma((n,)),
            dma((2, n, CHUNKS)),
            dma((n, CHUNKS)),
            dma((n // 2,)),
            dma((n // 2,)),
            dma((n // 2,)),
            dma((n_head,)),
            dma,
            dma,
        ],
        compiler_params=pltpu.CompilerParams(
            collective_id=0, has_side_effects=True, vmem_limit_bytes=60 * 2**20
        ),
    )(key_value, queries, out_weight)


def solution(mesh):
    assert mesh.shape["sub"] == 2
    assert mesh.shape["ctx"] == mesh.shape["head"] * mesh.shape["sub"]
    return jax.shard_map(
        on_device,
        mesh=mesh,
        in_specs=(
            P(("groups", "ctx"), ("head", "sub")),
            P(("groups", "ctx"), "head"),
            P(("groups", "ctx"), "head"),
            P(("head", "sub"), "ctx"),
        ),
        out_specs=P(("groups", "ctx"), ("head", "sub")),
        check_vma=False,
    )
```

time: 296 us -> 185 us (0.62)
  the two profiles are of different devices: /device:TPU:2 before, /device:TPU:3 now
where the time goes in v2:
time: 185 us; the launch traced here: 184 us
  Pallas kernels  180 us (97%)
  local copies, waits for them, and re-layouts  3.26 us (2%)
    pallas_call x1, Pallas kernels, on_device(): pl.pallas_call(functools.partial(kernel, n, n_head, per_pair, pairs), out...  180 us

profile of v2, /device:TPU:3, one launch (start us, length us, event | category | flops | bytes accessed | tf_op | source)
XLA Modules:
  0.0 184.5 jit_solution(12104242357046836374)
XLA Ops:
  0.0 1.0 constant_dynamic-slice_fusion
  1.1 0.8 pad_maximum_fusion.kv_ref
  1.8 180.4 %shard_map.46 = bf16[384,1280]{1,0:T(8,128)(2,1)} custom-call(bf16[384,512]{1,0:T(8,128)(2,1)} %pad_maximum_fusion.kv_ref, bf16[384,2048]{1,0:T(8,128)(2,1)} %q_ref.1, bf16[2048,1280]{1,0:T(8,128)(2,1)} %w_hbm.1), custom_call_target="tpu_custom_call" | custom-call | tf_op jit(solution)/shard_map/pallas_call | solution.py:247
  182.3 2.2 %copy.6 = bf16[384,1280]{1,0:T(8,128)(2,1)} copy(bf16[384,1280]{1,0:T(8,128)(2,1)} %shard_map.46) | data formatting | bytes 1966080

commit v3 on v2

v3 whole, which is shorter than its diff:
```python
import functools
import math

import jax
import jax.numpy as jnp
from jax import lax
from jax.experimental import pallas as pl
from jax.experimental.pallas import tpu as pltpu
from jax.sharding import PartitionSpec as P

QH = 64
KVH = 8
HD = 128
CHUNKS = 8
TILE = 256
ROWS = 128
MESH = pl.DeviceIdType.MESH


def kernel(
    n, n_head, per_pair, pairs, chunks, parts, k_hbm, v_hbm, q_hbm, w_hbm, o_ref,
    kv_all, v_ext, q_ref, att, w, own, out, rx1, summed, rx2, final,
    load_sems, kv_send, kv_recv, a_send, a_recv, s1, r1, s2, r2, s3, r3,
):
    me, head, sub = (lax.axis_index(a) for a in ("ctx", "head", "sub"))
    other = 1 - sub
    hs = head * 2 + sub
    tokens, width = q_ref.shape
    heads = width // HD
    columns = w.shape[1]
    piece = width // chunks
    to_right, to_left = me < n - 1, me > 0
    right, left = lax.min(me + 1, n - 1), lax.max(me - 1, 0)
    away = hs != me
    turned = {"ctx": hs, "head": me // 2, "sub": me % 2}

    def rows_of(b):
        return pl.ds(pl.multiple_of(b * tokens, tokens), tokens)

    first = pl.multiple_of((sub * heads // (QH // KVH)) * HD, HD)
    loads = [
        pltpu.make_async_copy(
            side.at[:, pl.ds(first, pairs * HD)],
            kv_all.at[rows_of(me), pl.ds(i * pairs * HD, pairs * HD)],
            load_sems.at[i],
        )
        for i, side in enumerate((k_hbm, v_hbm))
    ]
    loads.append(pltpu.make_async_copy(q_hbm, q_ref, load_sems.at[2]))
    loads.append(pltpu.make_async_copy(w_hbm, w, load_sems.at[3]))
    for load in loads:
        load.start()

    barrier = pltpu.get_barrier_semaphore()

    def greet(where):
        pl.semaphore_signal(barrier, inc=1, device_id=where, device_id_type=MESH)

    pl.when(to_right)(lambda: greet({"ctx": right}))
    pl.when(to_left)(lambda: greet({"ctx": left}))
    pl.when(away)(lambda: greet(turned))
    greet({"sub": other})
    for step in range(1, n_head):
        greet({"head": lax.rem(head + step, n_head)})
    count = n_head + to_right.astype(jnp.int32) + to_left.astype(jnp.int32)
    pl.semaphore_wait(barrier, count + away.astype(jnp.int32))

    def remote(src, dst, send, recv, where):
        return pltpu.make_async_remote_copy(
            src_ref=src, dst_ref=dst, send_sem=send, recv_sem=recv, device_id=where, device_id_type=MESH
        )

    def kv_copy(b, way, d):
        where = {"ctx": right if way == 0 else left}
        part = kv_all.at[rows_of(b)]
        return remote(part, part, kv_send.at[way, d], kv_recv.at[b], where)

    loads[0].wait()
    loads[1].wait()
    pl.when(to_right)(lambda: kv_copy(me, 0, 0).start())
    pl.when(to_left)(lambda: kv_copy(me, 1, 0).start())

    @pl.loop(1, n)
    def _(d):
        @pl.when(me - d >= 0)
        def _():
            copy = kv_copy(me - d, 0, d)
            copy.wait_recv()
            pl.when(to_right)(lambda: copy.start())

        @pl.when(me + d < n)
        def _():
            copy = kv_copy(me + d, 1, d)
            copy.wait_recv()
            pl.when(to_left)(lambda: copy.start())

    loads[2].wait()

    def a_copy(b, j, way, d):
        where = {"ctx": right if way == 0 else left}
        part = att.at[b, :, pl.ds(j * piece, piece)]
        return remote(part, part, a_send.at[way, d, j], a_recv.at[b, j], where)

    factor = math.log2(math.e) / HD**0.5
    for j in range(chunks):
        if j % (chunks // pairs) == 0:
            p = j // (chunks // pairs)
            v_ext[p, :, :HD] = kv_all[:, (pairs + p) * HD : (pairs + p + 1) * HD]
            v_ext[p, :, HD:] = jnp.ones((v_ext.shape[1], HD), v_ext.dtype)

        @pl.loop(j * heads // chunks, (j + 1) * heads // chunks)
        def _(h):
            pair = h // per_pair
            cols = pl.ds(pl.multiple_of(h * HD, HD), HD)
            keys = kv_all[:, pl.ds(pl.multiple_of(pair * HD, HD), HD)]
            for start in range(0, tokens, ROWS):
                rows = pl.ds(start, ROWS)
                scores = lax.dot_general(
                    q_ref[rows, cols], keys, (((1,), (1,)), ((), ())), preferred_element_type=jnp.float32
                )
                row_max = jnp.max(scores, axis=1, keepdims=True)
                weights = jnp.exp2((scores - row_max) * factor).astype(jnp.bfloat16)
                both = jnp.dot(weights, v_ext[pair], preferred_element_type=jnp.float32)
                att[me, rows, cols] = (both[:, :HD] / both[:, HD:]).astype(att.dtype)

        pl.when(to_right)(lambda: a_copy(me, j, 0, 0).start())
        pl.when(to_left)(lambda: a_copy(me, j, 1, 0).start())

    loads[3].wait()
    tile = columns // parts

    def cols_of(c):
        return pl.ds(0, columns) if parts == 1 else pl.ds(pl.multiple_of(c * tile, tile), tile)

    def core_copy(g, c):
        cols = cols_of(c)
        return remote(out.at[g, :, cols], rx1.at[g, :, cols], s1.at[g, c], r1.at[g, c], {"sub": other})

    def head_copy(g, c):
        cols = cols_of(c)
        return remote(
            summed.at[g, :, cols], rx2.at[head, :, cols], s2.at[g, c], r2.at[head, c], {"head": g}
        )

    def last_copy(c):
        cols = cols_of(c)
        return remote(final.at[:, cols], o_ref.at[:, cols], s3.at[c], r3.at[c], turned)

    def product(t, c):
        cols = cols_of(c)
        return jnp.dot(att[t], w[:, cols], preferred_element_type=jnp.float32).astype(out.dtype)

    def multiply(t):
        g = t // 2

        @pl.when(t % 2 == sub)
        def _():
            @pl.loop(0, parts)
            def _(c):
                own[g, :, cols_of(c)] = product(t, c)

        @pl.when(t % 2 != sub)
        def _():
            @pl.loop(0, parts)
            def _(c):
                out[g, :, cols_of(c)] = product(t, c)
                core_copy(g, c).start()

    def combine(t):
        g = t // 2

        @pl.when(t % 2 == sub)
        def _():
            @pl.loop(0, parts)
            def _(c):
                cols = cols_of(c)
                core_copy(g, c).wait_recv()
                total = own[g, :, cols].astype(jnp.float32) + rx1[g, :, cols].astype(jnp.float32)
                summed[g, :, cols] = total.astype(summed.dtype)
                pl.when(g != head)(lambda: head_copy(g, c).start())

    def finish():
        @pl.loop(0, parts)
        def _(c):
            cols = cols_of(c)
            total = summed[head, :, cols].astype(jnp.float32)
            for step in range(1, n_head):
                source = lax.rem(head + step, n_head)
                remote(
                    summed.at[source, :, cols], rx2.at[source, :, cols],
                    s2.at[source, c], r2.at[source, c], {"head": source},
                ).wait_recv()
                total += rx2[source, :, cols].astype(jnp.float32)
            final[:, cols] = total.astype(final.dtype)
            pl.when(away)(lambda: last_copy(c).start())

    gap = lax.max(hs - me, me - hs)

    def after(d, j, last=False):
        behind, ahead = me - d + 1, me + d - 1
        if j == 0:
            pl.when(behind >= 0)(lambda: multiply(behind))
        if j == chunks // 4:
            pl.when(jnp.logical_and(ahead < n, d > 1))(lambda: multiply(ahead))
        if j == chunks // 2:
            pl.when(behind >= 0)(lambda: combine(behind))
        if j == chunks // 2 + 1:
            pl.when(jnp.logical_and(ahead < n, d > 1))(lambda: combine(ahead))
        if j == chunks - 1 and not last:
            pl.when(gap == d - 2)(finish)

    @pl.loop(1, n)
    def _(d):
        for j in range(chunks):

            @pl.when(me - d >= 0)
            def _():
                copy = a_copy(me - d, j, 0, d)
                copy.wait_recv()
                pl.when(to_right)(lambda: copy.start())

            @pl.when(me + d < n)
            def _():
                copy = a_copy(me + d, j, 1, d)
                copy.wait_recv()
                pl.when(to_left)(lambda: copy.start())

            after(d, j)

    pl.when(gap == n - 2)(finish)
    for j in range(chunks):
        after(n, j, last=True)
    pl.when(gap == n - 1)(finish)

    @pl.when(away)
    def _():
        @pl.loop(0, parts)
        def _(c):
            last_copy(c).wait()

    @pl.when(jnp.logical_not(away))
    def _():
        keep = pltpu.make_async_copy(final, o_ref, load_sems.at[0])
        keep.start()
        keep.wait()

    @pl.loop(0, n)
    def _(d):
        for way, fits, go in ((0, me - d >= 0, to_right), (1, me + d < n, to_left)):
            b = me - d if way == 0 else me + d

            @pl.when(jnp.logical_and(fits, go))
            def _():
                kv_copy(b, way, d).wait_send()
                for j in range(chunks):
                    a_copy(b, j, way, d).wait_send()

    @pl.loop(0, n // 2)
    def _(g):
        @pl.loop(0, parts)
        def _(c):
            core_copy(g, c).wait_send()
            pl.when(g != head)(lambda: head_copy(g, c).wait_send())


def on_device(queries, key_rows, value_rows, out_weight):
    tokens, width = queries.shape
    heads_here = width // HD
    group_ratio = QH // KVH
    pairs = max(heads_here // group_ratio, 1)
    per_pair = heads_here // pairs
    n = lax.axis_size("ctx")
    n_head = lax.axis_size("head")
    columns = out_weight.shape[1]
    block = (tokens, columns)
    groups = (n // 2,) + block
    chunks = min(CHUNKS, heads_here)
    parts = columns // TILE if columns % TILE == 0 else 1
    anywhere = pl.BlockSpec(memory_space=pl.ANY)
    dma = pltpu.SemaphoreType.DMA
    bf16 = jnp.bfloat16
    return pl.pallas_call(
        functools.partial(kernel, n, n_head, per_pair, pairs, chunks, parts),
        out_shape=jax.ShapeDtypeStruct(block, bf16),
        in_specs=[anywhere] * 4,
        out_specs=anywhere,
        scratch_shapes=[
            pltpu.VMEM((n * tokens, 2 * pairs * HD), bf16),
            pltpu.VMEM((pairs, n * tokens, 2 * HD), bf16),
            pltpu.VMEM((tokens, width), bf16),
            pltpu.VMEM((n, tokens, width), bf16),
            pltpu.VMEM(out_weight.shape, bf16),
            pltpu.VMEM(groups, bf16),
            pltpu.VMEM(groups, bf16),
            pltpu.VMEM(groups, bf16),
            pltpu.VMEM(groups, bf16),
            pltpu.VMEM((n_head,) + block, bf16),
            pltpu.VMEM(block, bf16),
            dma((4,)),
            dma((2, n)),
            dma((n,)),
            dma((2, n, chunks)),
            dma((n, chunks)),
            dma((n // 2, parts)),
            dma((n // 2, parts)),
            dma((n // 2, parts)),
            dma((n_head, parts)),
            dma((parts,)),
            dma((parts,)),
        ],
        compiler_params=pltpu.CompilerParams(
            collective_id=0, has_side_effects=True, vmem_limit_bytes=60 * 2**20
        ),
    )(key_rows, value_rows, queries, out_weight)


def solution(mesh):
    assert mesh.shape["sub"] == 2
    assert mesh.shape["ctx"] == mesh.shape["head"] * mesh.shape["sub"]
    return jax.shard_map(
        on_device,
        mesh=mesh,
        in_specs=(
            P(("groups", "ctx"), ("head", "sub")),
            P(("groups", "ctx"), "head"),
            P(("groups", "ctx"), "head"),
            P(("head", "sub"), "ctx"),
        ),
        out_specs=P(("groups", "ctx"), ("head", "sub")),
        check_vma=False,
    )
```

time: 185 us -> 183 us (0.989)
  no operation moved by 1% of the time
where the time goes in v3:
time: 183 us
  Pallas kernels  181 us (99%)
  local copies, waits for them, and re-layouts  2.21 us (1%)
    pallas_call x1, Pallas kernels, on_device(): pl.pallas_call(functools.partial(kernel, n, n_head, per_pair, pairs, chun...  181 us

profile of v3, /device:TPU:3, one launch (start us, length us, event | category | flops | bytes accessed | tf_op | source)
XLA Modules:
  0.0 183.3 jit_solution(445212494998036470)
XLA Ops:
  0.0 181.1 %shard_map.46 = bf16[384,1280]{1,0:T(8,128)(2,1)} custom-call(bf16[384,512]{1,0:T(8,128)(2,1)} %k_hbm.1, bf16[384,512]{1,0:T(8,128)(2,1)} %v_hbm.1, bf16[384,2048]{1,0:T(8,128)(2,1)} %q_hbm.1, bf16[2048,1280]{1,0:T(8,128)(2,1)} %w_hbm.1), custom_call_target="tpu_custom_call" | custom-call | tf_op jit(solution)/shard_map/pallas_call | solution.py:282
  181.1 2.2 %copy.6 = bf16[384,1280]{1,0:T(8,128)(2,1)} copy(bf16[384,1280]{1,0:T(8,128)(2,1)} %shard_map.46) | data formatting | bytes 1966080

commit v4 on v3

--- a/solution.py
+++ b/solution.py
@@ -32,7 +32,7 @@
     to_right, to_left = me < n - 1, me > 0
     right, left = lax.min(me + 1, n - 1), lax.max(me - 1, 0)
     away = hs != me
-    turned = {"ctx": hs, "head": me // 2, "sub": me % 2}
+    share = tokens // n_head
 
     def rows_of(b):
         return pl.ds(pl.multiple_of(b * tokens, tokens), tokens)
@@ -58,11 +58,13 @@
 
     pl.when(to_right)(lambda: greet({"ctx": right}))
     pl.when(to_left)(lambda: greet({"ctx": left}))
-    pl.when(away)(lambda: greet(turned))
+    for h in range(n_head):
+        source = {"ctx": hs, "head": h, "sub": me % 2}
+        pl.when(jnp.logical_or(away, head != h))(functools.partial(greet, source))
     greet({"sub": other})
     for step in range(1, n_head):
         greet({"head": lax.rem(head + step, n_head)})
-    count = n_head + to_right.astype(jnp.int32) + to_left.astype(jnp.int32)
+    count = 2 * n_head - 1 + to_right.astype(jnp.int32) + to_left.astype(jnp.int32)
     pl.semaphore_wait(barrier, count + away.astype(jnp.int32))
 
     def remote(src, dst, send, recv, where):
@@ -136,15 +138,27 @@
         cols = cols_of(c)
         return remote(out.at[g, :, cols], rx1.at[g, :, cols], s1.at[g, c], r1.at[g, c], {"sub": other})
 
-    def head_copy(g, c):
+    def share_of(h):
+        return pl.ds(pl.multiple_of(h * share, share), share)
+
+    def head_copy(g, step, c):
+        cols, target = cols_of(c), lax.rem(head + step, n_head)
+        return remote(
+            summed.at[g, share_of(target), cols], rx2.at[g, head, :, cols],
+            s2.at[g, step - 1, c], r2.at[g, head, c], {"head": target},
+        )
+
+    def head_arrival(g, source, c):
         cols = cols_of(c)
         return remote(
-            summed.at[g, :, cols], rx2.at[head, :, cols], s2.at[g, c], r2.at[head, c], {"head": g}
+            summed.at[g, share_of(source), cols], rx2.at[g, source, :, cols],
+            s2.at[g, 0, c], r2.at[g, source, c], {"head": source},
         )
 
-    def last_copy(c):
+    def last_copy(g, h, c):
         cols = cols_of(c)
-        return remote(final.at[:, cols], o_ref.at[:, cols], s3.at[c], r3.at[c], turned)
+        where = {"ctx": 2 * g + sub, "head": me // 2, "sub": me % 2}
+        return remote(final.at[g, :, cols], o_ref.at[share_of(h), cols], s3.at[g, c], r3.at[h, c], where)
 
     def product(t, c):
         cols = cols_of(c)
@@ -177,24 +191,28 @@
                 core_copy(g, c).wait_recv()
                 total = own[g, :, cols].astype(jnp.float32) + rx1[g, :, cols].astype(jnp.float32)
                 summed[g, :, cols] = total.astype(summed.dtype)
-                pl.when(g != head)(lambda: head_copy(g, c).start())
-
-    def finish():
-        @pl.loop(0, parts)
-        def _(c):
-            cols = cols_of(c)
-            total = summed[head, :, cols].astype(jnp.float32)
-            for step in range(1, n_head):
-                source = lax.rem(head + step, n_head)
-                remote(
-                    summed.at[source, :, cols], rx2.at[source, :, cols],
-                    s2.at[source, c], r2.at[source, c], {"head": source},
-                ).wait_recv()
-                total += rx2[source, :, cols].astype(jnp.float32)
-            final[:, cols] = total.astype(final.dtype)
-            pl.when(away)(lambda: last_copy(c).start())
-
-    gap = lax.max(hs - me, me - hs)
+                for step in range(1, n_head):
+                    head_copy(g, step, c).start()
+
+    def finish(t):
+        g = t // 2
+
+        @pl.when(t % 2 == sub)
+        def _():
+            @pl.loop(0, parts)
+            def _(c):
+                cols = cols_of(c)
+                total = summed[g, share_of(head), cols].astype(jnp.float32)
+                for step in range(1, n_head):
+                    source = lax.rem(head + step, n_head)
+                    head_arrival(g, source, c).wait_recv()
+                    total += rx2[g, source, :, cols].astype(jnp.float32)
+                final[g, :, cols] = total.astype(final.dtype)
+                pl.when(jnp.logical_or(away, t != me))(lambda: last_copy(g, head, c).start())
+
+    def finish_at(d):
+        pl.when(jnp.logical_and(d >= 0, me - d >= 0))(lambda: finish(me - d))
+        pl.when(jnp.logical_and(d > 0, me + d < n))(lambda: finish(me + d))
 
     def after(d, j, last=False):
         behind, ahead = me - d + 1, me + d - 1
@@ -207,7 +225,7 @@
         if j == chunks // 2 + 1:
             pl.when(jnp.logical_and(ahead < n, d > 1))(lambda: combine(ahead))
         if j == chunks - 1 and not last:
-            pl.when(gap == d - 2)(finish)
+            finish_at(d - 2)
 
     @pl.loop(1, n)
     def _(d):
@@ -227,22 +245,24 @@
 
             after(d, j)
 
-    pl.when(gap == n - 2)(finish)
+    finish_at(n - 2)
     for j in range(chunks):
         after(n, j, last=True)
-    pl.when(gap == n - 1)(finish)
-
-    @pl.when(away)
-    def _():
-        @pl.loop(0, parts)
-        def _(c):
-            last_copy(c).wait()
+    finish_at(n - 1)
 
     @pl.when(jnp.logical_not(away))
     def _():
-        keep = pltpu.make_async_copy(final, o_ref, load_sems.at[0])
+        keep = pltpu.make_async_copy(final.at[me // 2], o_ref.at[share_of(head)], load_sems.at[0])
         keep.start()
         keep.wait()
+
+    for h in range(n_head):
+
+        @pl.when(jnp.logical_or(away, head != h))
+        def _():
+            @pl.loop(0, parts)
+            def _(c):
+                last_copy(0, h, c).wait_recv()
 
     @pl.loop(0, n)
     def _(d):
@@ -260,7 +280,9 @@
         @pl.loop(0, parts)
         def _(c):
             core_copy(g, c).wait_send()
-            pl.when(g != head)(lambda: head_copy(g, c).wait_send())
+            for step in range(1, n_head):
+                head_copy(g, step, c).wait_send()
+            pl.when(jnp.logical_or(away, 2 * g + sub != me))(lambda: last_copy(g, head, c).wait_send())
 
 
 def on_device(queries, key_rows, value_rows, out_weight):
@@ -294,8 +316,8 @@
             pltpu.VMEM(groups, bf16),
             pltpu.VMEM(groups, bf16),
             pltpu.VMEM(groups, bf16),
-            pltpu.VMEM((n_head,) + block, bf16),
-            pltpu.VMEM(block, bf16),
+            pltpu.VMEM((n // 2, n_head, tokens // n_head, columns), bf16),
+            pltpu.VMEM((n // 2, tokens // n_head, columns), bf16),
             dma((4,)),
             dma((2, n)),
             dma((n,)),
@@ -303,10 +325,10 @@
             dma((n, chunks)),
             dma((n // 2, parts)),
             dma((n // 2, parts)),
+            dma((n // 2, n_head - 1, parts)),
+            dma((n // 2, n_head, parts)),
             dma((n // 2, parts)),
             dma((n_head, parts)),
-            dma((parts,)),
-            dma((parts,)),
         ],
         compiler_params=pltpu.CompilerParams(
             collective_id=0, has_side_effects=True, vmem_limit_bytes=60 * 2**20

time: 183 us -> 167 us (0.913)
  Pallas kernels: 181 us -> 163 us
    pallas_call x1, Pallas kernels: 181 us -> 163 us  [on_device(): pl.pallas_call(functools.partial(kernel, n, n_head, per_pair, pairs, chun...]
where the time goes in v4:
time: 167 us; the launch traced here: 165 us
  Pallas kernels  163 us (98%)
  local copies, waits for them, and re-layouts  2.21 us (1%)
    pallas_call x1, Pallas kernels, on_device(): pl.pallas_call(functools.partial(kernel, n, n_head, per_pair, pairs, chun...  163 us

profile of v4, /device:TPU:3, one launch (start us, length us, event | category | flops | bytes accessed | tf_op | source)
XLA Modules:
  0.0 165.5 jit_solution(10364317827790260050)
XLA Ops:
  0.0 163.3 %shard_map.46 = bf16[384,1280]{1,0:T(8,128)(2,1)} custom-call(bf16[384,512]{1,0:T(8,128)(2,1)} %k_hbm.1, bf16[384,512]{1,0:T(8,128)(2,1)} %v_hbm.1, bf16[384,2048]{1,0:T(8,128)(2,1)} %q_hbm.1, bf16[2048,1280]{1,0:T(8,128)(2,1)} %w_hbm.1), custom_call_target="tpu_custom_call" | custom-call | tf_op jit(solution)/shard_map/pallas_call | solution.py:304
  163.3 2.2 %copy.6 = bf16[384,1280]{1,0:T(8,128)(2,1)} copy(bf16[384,1280]{1,0:T(8,128)(2,1)} %shard_map.46) | data formatting | bytes 1966080

commit v5 on v4

--- a/solution.py
+++ b/solution.py
@@ -210,9 +210,12 @@
                 final[g, :, cols] = total.astype(final.dtype)
                 pl.when(jnp.logical_or(away, t != me))(lambda: last_copy(g, head, c).start())
 
-    def finish_at(d):
-        pl.when(jnp.logical_and(d >= 0, me - d >= 0))(lambda: finish(me - d))
-        pl.when(jnp.logical_and(d > 0, me + d < n))(lambda: finish(me + d))
+    def finish_at(d, late):
+        for t, fits in ((me - d, d >= 0), (me + d, d > 0)):
+            at_end = jnp.logical_and(jnp.logical_or(t == 0, t == n - 1), t != me)
+            now = at_end if late else jnp.logical_not(at_end)
+            inside = jnp.logical_and(t >= 0, t < n)
+            pl.when(jnp.logical_and(jnp.logical_and(fits, inside), now))(functools.partial(finish, t))
 
     def after(d, j, last=False):
         behind, ahead = me - d + 1, me + d - 1
@@ -225,7 +228,7 @@
         if j == chunks // 2 + 1:
             pl.when(jnp.logical_and(ahead < n, d > 1))(lambda: combine(ahead))
         if j == chunks - 1 and not last:
-            finish_at(d - 2)
+            finish_at(d - 2, False)
 
     @pl.loop(1, n)
     def _(d):
@@ -245,10 +248,15 @@
 
             after(d, j)
 
-    finish_at(n - 2)
+    finish_at(n - 2, False)
+
+    @pl.loop(1, n - 1)
+    def _(d):
+        finish_at(d, True)
+
     for j in range(chunks):
         after(n, j, last=True)
-    finish_at(n - 1)
+    finish_at(n - 1, True)
 
     @pl.when(jnp.logical_not(away))
     def _():

time: 167 us -> 167 us (level)
  no operation moved by 1% of the time
where the time goes in v5:
time: 167 us; the launch traced here: 166 us
  Pallas kernels  163 us (98%)
  local copies, waits for them, and re-layouts  2.21 us (1%)
    pallas_call x1, Pallas kernels, on_device(): pl.pallas_call(functools.partial(kernel, n, n_head, per_pair, pairs, chun...  163 us

profile of v5, /device:TPU:3, one launch (start us, length us, event | category | flops | bytes accessed | tf_op | source)
XLA Modules:
  0.0 165.5 jit_solution(7024239597509502849)
XLA Ops:
  0.0 163.3 %shard_map.46 = bf16[384,1280]{1,0:T(8,128)(2,1)} custom-call(bf16[384,512]{1,0:T(8,128)(2,1)} %k_hbm.1, bf16[384,512]{1,0:T(8,128)(2,1)} %v_hbm.1, bf16[384,2048]{1,0:T(8,128)(2,1)} %q_hbm.1, bf16[2048,1280]{1,0:T(8,128)(2,1)} %w_hbm.1), custom_call_target="tpu_custom_call" | custom-call | tf_op jit(solution)/shard_map/pallas_call | solution.py:312
  163.3 2.2 %copy.6 = bf16[384,1280]{1,0:T(8,128)(2,1)} copy(bf16[384,1280]{1,0:T(8,128)(2,1)} %shard_map.46) | data formatting | bytes 1966080

commit v6 on v4

--- a/solution.py
+++ b/solution.py
@@ -11,7 +11,7 @@
 QH = 64
 KVH = 8
 HD = 128
-CHUNKS = 8
+CHUNKS = 16
 TILE = 256
 ROWS = 128
 MESH = pl.DeviceIdType.MESH

time: 167 us -> 168 us (level)
  Pallas kernels: 163 us -> 165 us
    pallas_call x1, Pallas kernels: 163 us -> 165 us  [on_device(): pl.pallas_call(functools.partial(kernel, n, n_head, per_pair, pairs, chun...]
where the time goes in v6:
time: 168 us; the launch traced here: 167 us
  Pallas kernels  165 us (98%)
  local copies, waits for them, and re-layouts  2.21 us (1%)
    pallas_call x1, Pallas kernels, on_device(): pl.pallas_call(functools.partial(kernel, n, n_head, per_pair, pairs, chun...  165 us

profile of v6, /device:TPU:3, one launch (start us, length us, event | category | flops | bytes accessed | tf_op | source)
XLA Modules:
  0.0 167.4 jit_solution(10309395246477384393)
XLA Ops:
  0.0 165.2 %shard_map.46 = bf16[384,1280]{1,0:T(8,128)(2,1)} custom-call(bf16[384,512]{1,0:T(8,128)(2,1)} %k_hbm.1, bf16[384,512]{1,0:T(8,128)(2,1)} %v_hbm.1, bf16[384,2048]{1,0:T(8,128)(2,1)} %q_hbm.1, bf16[2048,1280]{1,0:T(8,128)(2,1)} %w_hbm.1), custom_call_target="tpu_custom_call" | custom-call | tf_op jit(solution)/shard_map/pallas_call | solution.py:304
  165.2 2.2 %copy.6 = bf16[384,1280]{1,0:T(8,128)(2,1)} copy(bf16[384,1280]{1,0:T(8,128)(2,1)} %shard_map.46) | data formatting | bytes 1966080
